TPU v7x, 512 devices: a whole 4x4x16 slice. The times are simulated.
512 devices in a mesh: case: 8 (over x, core), elem: 64 (over y, z).
Axes of the slice: x: 4, y: 4, z: 16, core: 2. Of those that a mesh axis runs over, the one named last changes fastest.
Arguments:
- load_coef: bfloat16 [4096, 512], P(('case', 'elem')), may hold values from -13 to 13
- mantissa: bfloat16 [512, 3, 65536], P(None, None, 'elem'), may hold values from -0.25 to 0.25
- scale_exp: int32 [512, 3, 512], P(None, None, 'elem'), may hold values from -1 to 1
- lin_coef: float32 [2, 65536], P(None, 'elem'), may hold values from -0.5 to 0.5
- quad_coef: float32 [3, 65536], P(None, 'elem'), may hold values from 0.05 to 0.3
- cross_coef: float32 [65536], P('elem'), may hold values from -0.1 to 0.1
- ply_count: int32 [65536], P('elem'), may hold values from 0 to 7
- cotangent: float32 [4096], P('case'), may hold values from -6 to 6
Outputs:
- load_grad: float32 [4096, 512], P(('case', 'elem'))
- coef_grad: float32 [6, 65536], P(None, 'elem')
All inputs are finite; a program needn't handle non-finite values.
Results may differ from a plain program's by a relative error of at most 0.0065.
Values may be sent and summed in bfloat16 or wider, within the bound.
A program may use at most 64 MiB of HBM per device.

v0:
```python
import jax
import jax.numpy as jnp
from jax import lax
from jax.sharding import PartitionSpec as P

rho_value = 1.0


def per_device(
    load_coef, mantissa, scale_exp, lin_coef, quad_coef, cross_coef, ply_count, cotangent
):
    units, comps, width = mantissa.shape
    blocks = scale_exp.shape[2]
    factor = jnp.exp2(scale_exp.astype(jnp.float32)).astype(jnp.bfloat16)
    fields = (mantissa.reshape(units, comps, blocks, width // blocks) * factor[..., None]).reshape(
        units, comps * width
    )
    stress = jnp.dot(
        lax.all_gather(load_coef, "elem", axis=0, tiled=True),
        fields,
        preferred_element_type=jnp.float32,
    )
    first = stress[:, :width]
    second = stress[:, width : 2 * width]
    shear = stress[:, 2 * width :]
    plies = (ply_count + 1).astype(jnp.float32)
    index = (
        lin_coef[0] * first
        + lin_coef[1] * second
        + quad_coef[0] * first * first
        + quad_coef[1] * second * second
        + quad_coef[2] * shear * shear
        + 2.0 * cross_coef * first * second
    )
    local_peak = jnp.max(index, axis=1)
    peak = lax.pmax(local_peak, "elem")
    local_total = jnp.sum(plies * jnp.exp(rho_value * (index - peak[:, None])), axis=1)
    total = lax.psum(local_total, "elem")
    envelope = peak + jnp.log(total) / rho_value
    weight = cotangent[:, None] * plies * jnp.exp(rho_value * (index - envelope[:, None]))
    grad_one = weight * (lin_coef[0] + 2.0 * quad_coef[0] * first + 2.0 * cross_coef * second)
    grad_two = weight * (lin_coef[1] + 2.0 * quad_coef[1] * second + 2.0 * cross_coef * first)
    grad_three = weight * (2.0 * quad_coef[2] * shear)
    dstress = jnp.concatenate([grad_one, grad_two, grad_three], axis=1).astype(jnp.bfloat16)
    coef_local = jnp.stack(
        [
            jnp.sum(weight * first, axis=0),
            jnp.sum(weight * second, axis=0),
            jnp.sum(weight * first * first, axis=0),
            jnp.sum(weight * second * second, axis=0),
            jnp.sum(weight * shear * shear, axis=0),
            jnp.sum(weight * 2.0 * first * second, axis=0),
        ]
    )
    terms = lax.dot_general(
        dstress, fields, (((1,), (1,)), ((), ())), preferred_element_type=jnp.float32
    )
    load_grad = lax.psum_scatter(terms, "elem", scatter_dimension=0, tiled=True)
    coef_grad = lax.psum(coef_local, "case")
    return (load_grad, coef_grad)


def solution(mesh):
    return jax.shard_map(
        per_device,
        mesh=mesh,
        in_specs=(
            P(("case", "elem"), None),
            P(None, None, "elem"),
            P(None, None, "elem"),
            P(None, "elem"),
            P(None, "elem"),
            P("elem"),
            P("elem"),
            P("case"),
        ),
        out_specs=(P(("case", "elem"), None), P(None, "elem")),
        check_vma=False,
    )
```

profile of v0, /device:TPU:1, one launch (start us, length us, event | category | flops | bytes accessed | tf_op | source)
XLA Modules:
  0.0 1100.3 jit_solution(16444660311962095111)
XLA Ops:
  7.2 0.0 reduce-scatter.2.cloned.1.call-start
  7.2 0.7 broadcast_multiply_fusion.3
  7.9 0.7 add_convert_fusion
  8.6 0.8 fusion.14
  9.4 0.8 exponential_convert_fusion
  10.2 0.9 broadcast_multiply_fusion.2
  11.0 90.5 %all_gather.3 = bf16[512,512]{1,0:T(8,128)(2,1)} all-gather(bf16[8,512]{1,0:T(8,128)(2,1)} %param.8), channel_id=1, replica_groups=mesh['case'=8,'elem'=64] {'elem'}, dimensions={0}, use_global_device_ids=true | all-gather | bytes 532480 | tf_op jit(solution)/shard_map/all_gather | solution.py:19
  101.6 3.2 copy.11
  104.8 0.0 copy-start.3
  104.8 0.4 bitcast_multiply_fusion
  105.2 0.6 copy-done.3
  105.8 0.0 copy-start.1
  105.8 1.8 convolution_bitcast_fusion
  107.6 0.0 copy-done.1
  107.7 0.0 copy-start
  107.7 1.4 fusion.12
  109.1 1.2 copy-done
  110.3 0.0 copy-start.4
  110.3 112.3 %pmax.7 = f32[512]{0:T(512)S(1)} all-reduce(f32[512]{0:T(512)S(1)} %get-tuple-element.8), channel_id=1, replica_groups=mesh['case'=8,'elem'=64] {'elem'}, use_global_device_ids=true, to_apply=%region_1.0 | all-reduce | flops 512 | bytes 4096 | tf_op jit(solution)/shard_map/pmax | solution.py:36
  222.6 0.5 multiply_reduce_fusion.3
  223.2 110.8 %psum.14 = f32[512]{0:T(512)S(1)} all-reduce(f32[512]{0:T(512)S(1)} %multiply_reduce_fusion.3), channel_id=1, replica_groups=mesh['case'=8,'elem'=64] {'elem'}, use_global_device_ids=true, to_apply=%region_3.0 | all-reduce | flops 512 | bytes 4096 | tf_op jit(solution)/shard_map/psum | solution.py:38
  334.0 0.0 copy-done.4
  334.0 0.0 copy-start.2
  334.0 4.8 multiply_reduce_fusion
  338.8 0.0 copy-done.2
  338.8 2.8 fusion
  341.6 0.0 reduce-scatter.2.cloned.1.call-update
  341.6 0.1 stack.27
  341.6 101.8 %psum.15 = f32[6,1024]{1,0:T(8,128)} all-reduce(f32[6,1024]{1,0:T(8,128)S(1)} %stack.27), channel_id=1, replica_groups=mesh['case'=8,'elem'=64] {'case'}, use_global_device_ids=true, to_apply=%region_11.0 | all-reduce | flops 6144 | bytes 49152 | tf_op jit(solution)/shard_map/psum | solution.py:59
  443.5 650.0 %reduce-scatter.2.cloned.1.call-done = f32[8,512]{1,0:T(8,128)} async-done(((f32[512,512]{1,0:T(8,128)}), f32[8,512]{1,0:T(8,128)}) %reduce-scatter.2.cloned.1.call-update) | async-done | bytes 16400 | tf_op jit(solution)/shard_map/reduce_scatter | solution.py:58
  (1 shorter events, 0.0 us)
Async XLA Ops:
  7.2 1086.3 %reduce-scatter.2.cloned.1.call-start = ((), (), s32[]{:S(2)}) async-start(), calls=%async_computation.1 | async-start | bytes 1064960 | tf_op jit(solution)/shard_map/reduce_scatter | solution.py:58
  104.8 1.0 copy-start.3
  105.8 1.8 copy-start.1
  107.7 2.7 copy-start
  110.3 223.7 %copy-start.4 = (f32[512]{0:T(512)S(1)}, f32[512]{0:T(512)}, u32[]{:S(2)}) copy-start(f32[512]{0:T(512)} %param.15) | copy-start | bytes 6148
  334.0 4.8 copy-start.2
Sparse Core Ops, SparseCore 0:
  341.7 751.6 reduce-scatter.1
where the time goes:
time: 1110 us; the launch traced here: 1100 us
  waiting for transfers between devices  650 us (59%)
  blocking collectives  415 us (37%)
  between operations  14.1 us (1%)
    reduce_scatter x1, waiting for transfers between devices, per_device(): load_grad = lax.psum_scatter(terms, 'elem', scatter_dimension=0, tiled=True)  650 us
    pmax x1, blocking collectives, per_device(): peak = lax.pmax(local_peak, 'elem')  112 us
    psum x1, blocking collectives, per_device(): total = lax.psum(local_total, 'elem')  111 us
    psum x1, blocking collectives, per_device(): coef_grad = lax.psum(coef_local, 'case')  102 us
    all_gather x1, blocking collectives, per_device(): lax.all_gather(load_coef, 'elem', axis=0, tiled=True)  90.5 us
  transfers between devices with their start and end apart: 1, of which 1 were waited for; matrix products, arithmetic and copies ran while one was open for 0% of the time, Pallas kernels for 0%

commit v1 on v0

v1 whole, which is shorter than its diff:
```python
import jax
import jax.numpy as jnp
from jax import lax
from jax.experimental import pallas as pl
from jax.experimental.pallas import tpu as pltpu
from jax.sharding import PartitionSpec as P

MESH = pl.DeviceIdType.MESH
NZ = 16
NY = 4
NC = 8
ROWS = 8
CH = NZ * ROWS
U = 512
W = 1024
L = 128


def near_first(i):
    k = i // 2 + 1
    odd = lax.rem(i, 2)
    return k * (1 - odd) + (NZ - k) * odd


def kernel(
    coef_ref, mant_ref, exp_ref, lin_ref, quad_ref, cross_ref, ply_ref, cot_ref,
    grad_ref, cgrad_ref,
    cases, fields, stress, weight, dst, own, part, pull, zsum, zpart, zpull, facs, cpart,
    ystat, mstat, zstat,
    load_sem, home_sem, ag_s, ag_r, fw_s, fw_r, ys_s, ys_r, zs_s, zs_r, py_s, py_r, pz_s, pz_r, cg_s, cg_r,
):
    case = lax.axis_index("case")
    elem = lax.axis_index("elem")
    y = elem // NZ
    z = lax.rem(elem, NZ)

    def z_peer(d):
        return (case, y * NZ + lax.rem(z + d, NZ))

    def y_peer(d):
        return (case, lax.rem(y + d, NY) * NZ + z)

    def c_peer(d):
        return (lax.rem(case + d, NC), elem)

    def remote(src, dst_, s, r, dev):
        return pltpu.make_async_remote_copy(
            src_ref=src, dst_ref=dst_, send_sem=s, recv_sem=r, device_id=dev, device_id_type=MESH
        )

    load = pltpu.make_async_copy(mant_ref, fields, load_sem)
    load.start()

    barrier = pltpu.get_barrier_semaphore()

    def greet(n, peer):
        def body(d, c):
            pl.semaphore_signal(barrier, inc=1, device_id=peer(d), device_id_type=MESH)
            return c

        lax.fori_loop(1, n, body, 0)

    greet(NZ, z_peer)
    greet(NY, y_peer)
    greet(NC, c_peer)
    pl.semaphore_wait(barrier, NZ + NY + NC - 3)

    def rows_of(yy, zz):
        return pl.ds(pl.multiple_of((yy * NZ + zz) * ROWS, ROWS), ROWS)

    def chunk_of(yy):
        return pl.ds(pl.multiple_of(yy * CH, CH), CH)

    def ag_copy(d):
        return remote(coef_ref, cases.at[rows_of(y, z)], ag_s.at[d], ag_r.at[d], z_peer(d))

    def ag_send(i, c):
        ag_copy(near_first(NZ - 2 - i)).start()
        return c

    lax.fori_loop(0, NZ - 1, ag_send, 0)
    home = pltpu.make_async_copy(coef_ref, cases.at[rows_of(y, z)], home_sem)
    home.start()

    def forward(src, zz):
        for d in (2, 1, 3):
            remote(src, cases.at[rows_of(y, zz)], fw_s.at[d], fw_r.at[d], y_peer(d)).start()

    forward(coef_ref, z)

    load.wait()
    eye = lax.broadcasted_iota(jnp.int32, (L, L), 0) == lax.broadcasted_iota(jnp.int32, (L, L), 1)

    def column(row):
        return jnp.sum(jnp.where(eye, jnp.broadcast_to(row, (L, L)), 0.0), axis=1, keepdims=True)

    def as_row(col):
        return jnp.sum(jnp.where(eye, jnp.broadcast_to(col, (L, L)), 0.0), axis=0, keepdims=True)

    for k in range(3):
        def scale(b, c, k=k):
            lanes = pl.ds(pl.multiple_of(b * L, L), L)
            gains = jnp.exp2(exp_ref[k, pl.ds(b, 1), :].astype(jnp.float32))
            for r in range(U // L):
                gain = column(gains[:, r * L : (r + 1) * L])
                block = fields[k, r * L : (r + 1) * L, lanes].astype(jnp.float32)
                fields[k, r * L : (r + 1) * L, lanes] = (block * gain).astype(jnp.bfloat16)
            return c

        lax.fori_loop(0, W // L, scale, 0)

    home.wait()

    def ag_take(i, c):
        d = near_first(i)
        zz = lax.rem(z + NZ - d, NZ)
        remote(coef_ref, cases.at[rows_of(y, zz)], ag_s.at[d], ag_r.at[d], z_peer(d)).wait_recv()
        forward(cases.at[rows_of(y, zz)], zz)
        return c

    lax.fori_loop(0, NZ - 1, ag_take, 0)

    def chunk(q, c):
        dy = q + (q // 2) * (5 - 2 * q)
        src = lax.rem(y + NY - dy, NY)
        rows = chunk_of(src)
        back = lax.rem(NY - dy, NY)

        @pl.when(q > 0)
        def _():
            remote(cases.at[rows], cases.at[rows], fw_s.at[dy], fw_r.at[dy], y_peer(dy)).wait_recv()

        a = cases[rows, :]
        for k in range(3):
            stress[k, rows, :] = jnp.dot(a, fields[k], preferred_element_type=jnp.float32)

        def index_of(j, top):
            lanes = pl.ds(pl.multiple_of(j * L, L), L)
            s1 = stress[0, rows, lanes]
            s2 = stress[1, rows, lanes]
            t = stress[2, rows, lanes]
            one = lin_ref[0:1, lanes] + quad_ref[0:1, lanes] * s1 + (2.0 * cross_ref[0:1, lanes]) * s2
            two = lin_ref[1:2, lanes] + quad_ref[1:2, lanes] * s2
            index = s1 * one + s2 * two + quad_ref[2:3, lanes] * (t * t)
            weight[rows, lanes] = index
            return jnp.maximum(top, index)

        top = lax.fori_loop(0, W // L, index_of, jnp.full((CH, L), -jnp.inf, jnp.float32))
        peak = jnp.max(top, axis=1, keepdims=True)

        def weigh(j, total):
            lanes = pl.ds(pl.multiple_of(j * L, L), L)
            s1 = stress[0, rows, lanes]
            s2 = stress[1, rows, lanes]
            t = stress[2, rows, lanes]
            plies = (ply_ref[0:1, lanes] + 1).astype(jnp.float32)
            w = plies * jnp.exp(weight[rows, lanes] - peak)
            weight[rows, lanes] = w
            f12 = 2.0 * cross_ref[0:1, lanes]
            dst[0, :, lanes] = (
                w * (lin_ref[0:1, lanes] + (2.0 * quad_ref[0:1, lanes]) * s1 + f12 * s2)
            ).astype(jnp.bfloat16)
            dst[1, :, lanes] = (
                w * (lin_ref[1:2, lanes] + (2.0 * quad_ref[1:2, lanes]) * s2 + f12 * s1)
            ).astype(jnp.bfloat16)
            dst[2, :, lanes] = (w * ((2.0 * quad_ref[2:3, lanes]) * t)).astype(jnp.bfloat16)
            return total + w

        total = lax.fori_loop(0, W // L, weigh, jnp.zeros((CH, L), jnp.float32))
        total = jnp.sum(total, axis=1, keepdims=True)
        ystat[0, pl.ds(src, 1), :] = as_row(peak)
        ystat[0, pl.ds(NY + src, 1), :] = as_row(total)

        @pl.when(q == NY - 1)
        def _():
            for d in (2, 1, 3):
                remote(ystat.at[0], ystat.at[d], ys_s.at[d], ys_r.at[d], y_peer(d)).start()

        terms = sum(
            lax.dot_general(
                dst[k], fields[k], (((1,), (1,)), ((), ())), preferred_element_type=jnp.float32
            )
            for k in range(3)
        )

        @pl.when(q == 0)
        def _():
            own[...] = terms

        @pl.when(q > 0)
        def _():
            part[back] = terms.astype(jnp.bfloat16)
            remote(part.at[back], pull.at[back], py_s.at[back], py_r.at[back], y_peer(back)).start()

        return c

    lax.fori_loop(0, NY, chunk, 0)

    for d in (1, 3, 2):
        remote(ystat.at[0], ystat.at[d], ys_s.at[d], ys_r.at[d], y_peer(d)).wait_recv()
    mid = jnp.max(ystat[:, 0:NY, :], axis=0)
    mstat[0:NY, :] = mid
    mstat[NY:, :] = jnp.sum(ystat[:, NY:, :] * jnp.exp(ystat[:, 0:NY, :] - mid[None]), axis=0)
    zstat[0] = mstat[...]

    def zs_copy(d):
        return remote(mstat, zstat.at[d], zs_s.at[d], zs_r.at[d], z_peer(d))

    def zs_send(i, c):
        zs_copy(near_first(NZ - 2 - i)).start()
        return c

    lax.fori_loop(0, NZ - 1, zs_send, 0)

    mid_y = mstat[pl.ds(y, 1), :]

    def share(d):
        return column(jnp.exp(ystat[d, pl.ds(y, 1), :] - mid_y))

    merged = own[...] * share(0)
    for d in (1, 3, 2):
        remote(part.at[d], pull.at[d], py_s.at[d], py_r.at[d], y_peer(d)).wait_recv()
        merged = merged + pull[d].astype(jnp.float32) * share(d)
    merged = merged.reshape(NZ, ROWS, U)
    zsum[...] = merged
    zpart[...] = merged.astype(jnp.bfloat16)

    def pz_copy(d):
        return remote(
            zpart.at[lax.rem(z + d, NZ)], zpull.at[d], pz_s.at[d], pz_r.at[d], z_peer(d)
        )

    def pz_send(i, c):
        pz_copy(near_first(NZ - 2 - i)).start()
        return c

    lax.fori_loop(0, NZ - 1, pz_send, 0)

    def zs_take(d, c):
        zs_copy(d).wait_recv()
        return c

    lax.fori_loop(1, NZ, zs_take, 0)
    peak = jnp.max(zstat[:, 0:NY, :], axis=0)
    total = jnp.sum(zstat[:, NY:, :] * jnp.exp(zstat[:, 0:NY, :] - peak[None]), axis=0)
    cot = cot_ref[...] / total
    factor = cot * jnp.exp(ystat[0, 0:NY, :] - peak)
    for r in range(NY):
        facs[r * L : (r + 1) * L, :] = jnp.broadcast_to(column(factor[r : r + 1, :]), (L, L))

    def coefs(j, c):
        lanes = pl.ds(pl.multiple_of(j * L, L), L)
        acc = [jnp.zeros((8, L), jnp.float32) for _ in range(6)]
        for r in range(NY):
            rows = slice(r * L, (r + 1) * L)
            w = weight[rows, lanes] * facs[rows, :]
            s1 = stress[0, rows, lanes]
            s2 = stress[1, rows, lanes]
            t = stress[2, rows, lanes]
            w1 = w * s1
            w2 = w * s2
            for n, v in enumerate((w1, w2, w1 * s1, w2 * s2, w * t * t, w1 * (2.0 * s2))):
                acc[n] = acc[n] + jnp.sum(v.reshape(L // 8, 8, L), axis=0)
        for n in range(6):
            cpart[case, n : n + 1, lanes] = jnp.sum(acc[n], axis=0, keepdims=True)
        return c

    lax.fori_loop(0, W // L, coefs, 0)

    def cg_copy(d):
        return remote(cpart.at[case], cpart.at[case], cg_s.at[d], cg_r.at[d], c_peer(d))

    for d in (4, 3, 5, 2, 6, 1, 7):
        cg_copy(d).start()

    pick = lax.broadcasted_iota(jnp.int32, (ROWS, L), 1) == z * ROWS + lax.broadcasted_iota(
        jnp.int32, (ROWS, L), 0
    )
    gain_y = jnp.sum(jnp.where(lax.broadcasted_iota(jnp.int32, (NY, L), 0) == y, cot, 0.0), axis=0, keepdims=True)
    peak_y = jnp.sum(jnp.where(lax.broadcasted_iota(jnp.int32, (NY, L), 0) == y, peak, 0.0), axis=0, keepdims=True)

    def gain(d):
        row = gain_y * jnp.exp(zstat[d, pl.ds(y, 1), :] - peak_y)
        return jnp.sum(jnp.where(pick, jnp.broadcast_to(row, (ROWS, L)), 0.0), axis=1, keepdims=True)

    def pz_take(i, acc):
        d = near_first(i)
        pz_copy(d).wait_recv()
        return acc + zpull[d].astype(jnp.float32) * gain(d)

    grad_ref[...] = lax.fori_loop(0, NZ - 1, pz_take, zsum[z] * gain(0))

    for d in range(1, NC):
        src = lax.rem(case + NC - d, NC)
        remote(cpart.at[src], cpart.at[src], cg_s.at[d], cg_r.at[d], c_peer(d)).wait_recv()
    cgrad_ref[...] = jnp.sum(cpart[...], axis=0)

    def sent(d, c):
        ag_copy(d).wait_send()
        zs_copy(d).wait_send()
        pz_copy(d).wait_send()
        return c

    lax.fori_loop(1, NZ, sent, 0)
    rows = chunk_of(y)
    for d in range(1, NY):
        remote(cases.at[rows], cases.at[rows], fw_s.at[d], fw_r.at[d], y_peer(d)).wait_send()
        remote(ystat.at[0], ystat.at[d], ys_s.at[d], ys_r.at[d], y_peer(d)).wait_send()
        remote(part.at[d], pull.at[d], py_s.at[d], py_r.at[d], y_peer(d)).wait_send()
    for d in range(1, NC):
        cg_copy(d).wait_send()


def per_device(load_coef, mantissa, scale_exp, lin_coef, quad_coef, cross_coef, ply_count, cotangent):
    f32, bf16 = jnp.float32, jnp.bfloat16
    vmem = pl.BlockSpec(memory_space=pltpu.VMEM)
    dma = pltpu.SemaphoreType.DMA
    return pl.pallas_call(
        kernel,
        out_shape=(
            jax.ShapeDtypeStruct((ROWS, U), f32),
            jax.ShapeDtypeStruct((6, W), f32),
        ),
        in_specs=[vmem, pl.BlockSpec(memory_space=pl.ANY)] + [vmem] * 6,
        out_specs=(vmem, vmem),
        scratch_shapes=[
            pltpu.VMEM((NY * CH, U), bf16),
            pltpu.VMEM((3, U, W), bf16),
            pltpu.VMEM((3, NY * CH, W), f32),
            pltpu.VMEM((NY * CH, W), f32),
            pltpu.VMEM((3, CH, W), bf16),
            pltpu.VMEM((CH, U), f32),
            pltpu.VMEM((NY, CH, U), bf16),
            pltpu.VMEM((NY, CH, U), bf16),
            pltpu.VMEM((NZ, ROWS, U), f32),
            pltpu.VMEM((NZ, ROWS, U), bf16),
            pltpu.VMEM((NZ, ROWS, U), bf16),
            pltpu.VMEM((NY * CH, L), f32),
            pltpu.VMEM((NC, 6, W), f32),
            pltpu.VMEM((NY, 2 * NY, L), f32),
            pltpu.VMEM((2 * NY, L), f32),
            pltpu.VMEM((NZ, 2 * NY, L), f32),
            dma, dma, dma((NZ,)), dma((NZ,)), dma((NY,)), dma((NY,)), dma((NY,)), dma((NY,)),
            dma((NZ,)), dma((NZ,)), dma((NY,)), dma((NY,)), dma((NZ,)), dma((NZ,)), dma((NC,)), dma((NC,)),
        ],
        compiler_params=pltpu.CompilerParams(
            collective_id=0, has_side_effects=True, vmem_limit_bytes=56 << 20
        ),
        name="envelope_grad",
    )(
        load_coef,
        jnp.transpose(mantissa, (1, 0, 2)),
        jnp.transpose(scale_exp, (1, 2, 0)),
        lin_coef,
        quad_coef,
        cross_coef.reshape(1, -1),
        ply_count.reshape(1, -1),
        cotangent.reshape(NY, L),
    )


def solution(mesh):
    return jax.shard_map(
        per_device,
        mesh=mesh,
        in_specs=(
            P(("case", "elem"), None),
            P(None, None, "elem"),
            P(None, None, "elem"),
            P(None, "elem"),
            P(None, "elem"),
            P("elem"),
            P("elem"),
            P("case"),
        ),
        out_specs=(P(("case", "elem"), None), P(None, "elem")),
        check_vma=False,
    )
```

time: 1110 us -> 64.2 us (0.06)
  waiting for transfers between devices: 650 us -> 0 us
  blocking collectives: 415 us -> 0 us
  Pallas kernels: 0 us -> 60.5 us
  between operations: 14.1 us -> 0.64 us
    reduce_scatter x1 -> x0, waiting for transfers between devices: 650 us -> none  [per_device(): load_grad = lax.psum_scatter(terms, 'elem', scatter_dimension=0, tiled=True)]
    psum x2 -> x0, blocking collectives: 213 us -> none  [the longest x1 111 us: per_device(): total = lax.psum(local_total, 'elem')]
    pmax x1 -> x0, blocking collectives: 112 us -> none  [per_device(): peak = lax.pmax(local_peak, 'elem')]
    all_gather x1 -> x0, blocking collectives: 90.5 us -> none  [per_device(): lax.all_gather(load_coef, 'elem', axis=0, tiled=True)]
    pallas_call x0 -> x1, Pallas kernels: none -> 60.5 us  [per_device(): pl.pallas_call(kernel, out_shape=(jax.ShapeDtypeStruct((ROWS, U), f32), j...]
  transfers between devices with their start and end apart: 1 -> 0, of which waited for: 1 -> 0; matrix products, arithmetic and copies ran while one was open for 0% -> 0% of each run, Pallas kernels for 0% -> 0%
where the time goes in v1:
time: 64.2 us; the launch traced here: 63.9 us
  Pallas kernels  60.5 us (94%)
  local copies, waits for them, and re-layouts  2.7 us (4%)
    pallas_call x1, Pallas kernels, per_device(): pl.pallas_call(kernel, out_shape=(jax.ShapeDtypeStruct((ROWS, U), f32), j...  60.5 us
    unnamed x2, local copies, waits for them, and re-layouts  2.7 us

profile of v1, /device:TPU:1, one launch (start us, length us, event | category | flops | bytes accessed | tf_op | source)
XLA Modules:
  0.0 63.9 jit_solution(15936344226770249860)
XLA Ops:
  0.6 60.5 %envelope_grad.1 = (f32[8,512]{1,0:T(8,128)}, f32[6,1024]{1,0:T(8,128)}) custom-call(bf16[8,512]{1,0:T(8,128)(2,1)} %coef_ref.1, bf16[3,512,1024]{2,1,0:T(8,128)(2,1)} %bitcast.5, s32[3,8,512]{2,1,0:T(8,128)} %bitcast.6, f32[2,1024]{1,0:T(2,128)} %lin_ref.1, f32[3,1024]{1,0:T(4,128)} %quad_ref.1, f32[1,1024]{1,0:T(1,128)} %bitcast.7, s32[1,1024]{1,0:T(1,128)} %bitcast.8, ...), custom_call_target="tpu_custom_call" | custom-call | tf_op jit(solution)/shard_map/envelope_grad/pallas_call | solution.py:318
  61.2 1.3 %copy.12 = f32[8,512]{1,0:T(8,128)} copy(f32[8,512]{1,0:T(8,128)} %get-tuple-element.4) | data formatting | bytes 32768
  62.5 1.4 %copy.13 = f32[6,1024]{1,0:T(8,128)} copy(f32[6,1024]{1,0:T(8,128)} %get-tuple-element.5) | data formatting | bytes 49152
